TPU v7x, 256 devices: a whole 4x4x8 slice. The times are simulated.
256 devices in a mesh: frame: 32 (over y, x, core), space: 8 (over z).
Axes of the slice: x: 4, y: 4, z: 8, core: 2. Of those that a mesh axis runs over, the one named last changes fastest.
Arguments:
- query_tokens: bfloat16 [32, 2048, 2240], P('frame', 'space'), may hold values from -6 to 6
- key_tokens: bfloat16 [32, 2048, 2240], P('frame', 'space'), may hold values from -500 to 500
- value_tokens: bfloat16 [32, 2048, 2240], P('frame', 'space'), may hold values from -6 to 6
- out_grad: bfloat16 [32, 2048, 2240], P('frame', 'space'), may hold values from -768 to 768
Outputs:
- query_grad: float32 [32, 2048, 2240], P('frame', 'space')
- key_grad: float32 [32, 2048, 2240], P('frame', 'space')
- value_grad: float32 [32, 2048, 2240], P('frame', 'space')
All inputs are finite; a program needn't handle non-finite values.
Results may differ from a plain program's by a relative error of at most 0.0041.
Values sent between devices are 32-bit elements; how exact they have to be, the bound alone decides.
No kernel may reach another device: no remote copies, remote signals or barrier semaphores. Data moves between devices by JAX's collectives and lax.ppermute only.
A program may use at most 128 MiB of HBM per device.

v0:
```python
import jax
import jax.numpy as jnp
from jax import lax
from jax.sharding import PartitionSpec as P

HEADS = 20
HEAD_DIM = 112


HIGH = lax.Precision.HIGHEST


def entering(array, axis, combine, identity, reverse):
    devices, position = (lax.axis_size(axis), lax.axis_index(axis))
    everything = jax.tree.map(lambda part: lax.all_gather(part, axis), array)
    start = jax.tree.map(
        lambda part, zero: jnp.broadcast_to(jnp.asarray(zero, part.dtype), part.shape),
        array,
        identity,
    )

    def lap(k, before):
        at = devices - 1 - k if reverse else k
        reached = at > position if reverse else at < position
        new = combine(before, jax.tree.map(lambda part: part[at], everything))
        return jax.tree.map(lambda a, b: jnp.where(reached, a, b), new, before)

    return lax.fori_loop(0, devices, lap, start)


def add_pair(earlier, later):
    return (earlier[0] + later[0], earlier[1] + later[1])


def prefix_states(local_state, local_z):
    totals = lax.psum((local_state, local_z), "space")
    blank = (jnp.zeros_like(totals[0]), jnp.zeros_like(totals[1]))
    before = entering(totals, "frame", add_pair, blank, False)
    return add_pair(before, totals)


def suffix_grads(local_grad, local_zgrad):
    totals = lax.psum((local_grad, local_zgrad), "space")
    blank = (jnp.zeros_like(totals[0]), jnp.zeros_like(totals[1]))
    after = entering(totals, "frame", add_pair, blank, True)
    return add_pair(after, totals)


def on_device(query_tokens, key_tokens, value_tokens, out_grad):
    tile_rows = query_tokens.shape[1]
    q_heads = query_tokens.reshape(tile_rows, HEADS, HEAD_DIM)
    k_heads = key_tokens.reshape(tile_rows, HEADS, HEAD_DIM)
    v_heads = value_tokens.reshape(tile_rows, HEADS, HEAD_DIM)
    q_feat = jnp.maximum(q_heads, 0)
    k_feat = jnp.maximum(k_heads, 0)
    local_state = jnp.einsum("thi,thj->ihj", k_feat, v_heads, preferred_element_type=jnp.float32)
    local_z = jnp.sum(k_feat, axis=0, dtype=jnp.float32).T
    state_flat, zsum = prefix_states(local_state.reshape(HEAD_DIM, HEADS * HEAD_DIM), local_z)
    state = state_flat.reshape(HEAD_DIM, HEADS, HEAD_DIM)
    q_wide = q_feat.astype(jnp.float32)
    out_heads = out_grad.reshape(tile_rows, HEADS, HEAD_DIM).astype(jnp.float32)
    numerator = jnp.einsum("thi,ihj->thj", q_wide, state, precision=HIGH)
    denominator = jnp.einsum("thi,ih->th", q_wide, zsum, precision=HIGH) + 1.0
    scaled_low = (out_heads / denominator[:, :, None]).astype(jnp.bfloat16)
    scaled = lax.optimization_barrier(scaled_low).astype(jnp.float32)
    denom_grad = -jnp.sum(out_heads * numerator, axis=-1) / (denominator * denominator)
    direct = jnp.einsum("thj,ihj->thi", scaled, state, precision=HIGH)
    query_grad = jnp.where(q_heads > 0, direct + denom_grad[:, :, None] * zsum.T[None], 0.0)
    local_grad = jnp.einsum("thi,thj->ihj", q_feat, scaled_low, preferred_element_type=jnp.float32)
    local_zgrad = jnp.einsum("thi,th->ih", q_wide, denom_grad, precision=HIGH)
    grad_flat, zsum_grad = suffix_grads(local_grad.reshape(HEAD_DIM, HEADS * HEAD_DIM), local_zgrad)
    state_grad = grad_flat.reshape(HEAD_DIM, HEADS, HEAD_DIM)
    k_wide = k_feat.astype(jnp.float32)
    v_wide = v_heads.astype(jnp.float32)
    value_grad = jnp.einsum("thi,ihj->thj", k_wide, state_grad, precision=HIGH)
    key_part = jnp.einsum("thj,ihj->thi", v_wide, state_grad, precision=HIGH)
    key_grad = jnp.where(k_heads > 0, key_part + zsum_grad.T[None], 0.0)
    width_all = HEADS * HEAD_DIM
    return (
        query_grad.reshape(1, tile_rows, width_all),
        key_grad.reshape(1, tile_rows, width_all),
        value_grad.reshape(1, tile_rows, width_all),
    )


def solution(mesh):
    placed = (
        P("frame", "space", None),
        P("frame", "space", None),
        P("frame", "space", None),
        P("frame", "space", None),
    )
    return jax.shard_map(
        on_device,
        mesh=mesh,
        in_specs=placed,
        out_specs=(P("frame", "space", None), P("frame", "space", None), P("frame", "space", None)),
        check_vma=False,
    )
```

profile of v0, /device:TPU:1, one launch (start us, length us, event | category | flops | bytes accessed | tf_op | source)
XLA Modules:
  0.0 570.1 jit_solution(222670889405435051)
XLA Ops:
  11.6 76.1 %all-reduce.3.cloned.1.call-done = f32[112,2240]{0,1:T(8,128)} async-done(((f32[112,2240]{0,1:T(8,128)}), f32[112,2240]{0,1:T(8,128)}) %all-reduce.3.cloned.1.call-update) | async-done | bytes 1003536 | tf_op jit(solution)/shard_map/psum | solution.py:36
  87.7 2.6 copy.27
  90.9 22.0 %psum.29 = f32[112,20]{0,1:T(8,128)S(1)} all-reduce(f32[112,20]{0,1:T(8,128)S(1)} %bitcast.111), channel_id=1, replica_groups=mesh['frame'=32,'space'=8] {'space'}, use_global_device_ids=true, to_apply=%region_2.0 | all-reduce | flops 2240 | bytes 17920 | tf_op jit(solution)/shard_map/psum | solution.py:36
  112.9 39.3 %all-gather.4 = f32[32,112,20]{1,2,0:T(8,128)} all-gather(f32[1,112,20]{1,2,0:T(8,128)S(1)} %bitcast.110), channel_id=3, replica_groups=mesh['frame'=32,'space'=8] {'frame'}, dimensions={0}, use_global_device_ids=true | all-gather | bytes 295680 | tf_op jit(solution)/shard_map/all_gather | solution.py:15
  153.6 58.8 %all-gather.9.cloned.1.call-done = f32[3584,2240]{1,0:T(8,128)} async-done(((f32[112,2240]{1,0:T(8,128)}), f32[3584,2240]{1,0:T(8,128)}) %all-gather.9.cloned.1.call-update) | async-done | bytes 32112656 | tf_op jit(solution)/shard_map/all_gather | solution.py:15
  212.4 71.6 %while.34 = (s32[]{:T(128)}, f32[112,2240]{1,0:T(8,128)S(1)}, f32[112,20]{0,1:T(8,128)S(1)}, s32[]{:T(128)}, f32[32,112,2240]{2,1,0:T(8,128)}, /*index=5*/f32[32,112,20]{1,2,0:T(8,128)}, s32[]{:T(128)}, s32[]{:T(128)}) while((s32[]{:T(128)}, f32[112,2240]{1,0:T(8,128)S(1)}, f32[112,20]{0,1:T(8,128)S(1)}, s32[]{:T(128)}, ...), condition=%wide.region_4.5_spmd.clone, body=%wide.region_3.4_spmd.clone.sunk | while | flops 759364 | bytes 3037555 | solution.py:28
  212.4 1.5 add_select_fusion.8
  214.6 1.5 add_select_fusion.8
  219.1 1.5 add_select_fusion.8
  221.3 1.5 add_select_fusion.8
  223.6 1.5 add_select_fusion.8
  225.8 1.5 add_select_fusion.8
  230.3 1.5 add_select_fusion.8
  232.5 1.5 add_select_fusion.8
  234.7 1.5 add_select_fusion.8
  237.0 1.5 add_select_fusion.8
  241.4 1.5 add_select_fusion.8
  243.7 1.5 add_select_fusion.8
  245.9 1.5 add_select_fusion.8
  287.0 2.6 copy.30
  289.6 70.6 %all-reduce.5.cloned.1.call-done = f32[112,2240]{1,0:T(8,128)} async-done(((f32[112,2240]{1,0:T(8,128)}), f32[112,2240]{1,0:T(8,128)}) %all-reduce.5.cloned.1.call-update) | async-done | bytes 1003536 | tf_op jit(solution)/shard_map/psum | solution.py:43
  360.3 2.5 broadcast_compare_fusion
  365.3 1.9 add.130
  369.9 23.1 %psum.31 = f32[112,20]{0,1:T(8,128)S(1)} all-reduce(f32[112,20]{0,1:T(8,128)S(1)} %bitcast.112), channel_id=1, replica_groups=mesh['frame'=32,'space'=8] {'space'}, use_global_device_ids=true, to_apply=%region_7.8 | all-reduce | flops 2240 | bytes 17920 | tf_op jit(solution)/shard_map/psum | solution.py:43
  393.0 38.9 %all-gather.5 = f32[32,112,20]{1,2,0:T(8,128)} all-gather(f32[1,112,20]{1,2,0:T(8,128)S(1)} %bitcast.109), channel_id=5, replica_groups=mesh['frame'=32,'space'=8] {'frame'}, dimensions={0}, use_global_device_ids=true | all-gather | bytes 295680 | tf_op jit(solution)/shard_map/all_gather | solution.py:15
  431.9 4.5 fusion.2
  436.4 47.4 %all-gather.11.cloned.1.call-done = f32[3584,2240]{1,0:T(8,128)} async-done(((f32[112,2240]{1,0:T(8,128)}), f32[3584,2240]{1,0:T(8,128)}) %all-gather.11.cloned.1.call-update) | async-done | bytes 32112656 | tf_op jit(solution)/shard_map/all_gather | solution.py:15
  483.9 71.7 %while.35 = (s32[]{:T(128)}, f32[112,2240]{1,0:T(8,128)S(1)}, f32[112,20]{0,1:T(8,128)S(1)}, s32[]{:T(128)}, f32[32,112,2240]{2,1,0:T(8,128)}, /*index=5*/f32[32...) while((s32[]{:T(128)}, f32[112,2240]{1,0:T(8,128)S(1)}, ...), condition=%wide.region_9.10_spmd.clone, body=%wide.region_8.9_spmd.clone.sunk | while | flops 759368 | bytes 3037617 | solution.py:28
  483.9 1.6 add_select_fusion.10
  556.6 1.7 copy.31
  558.3 2.4 fusion.9
  560.7 2.8 bitcast_select_fusion
  (173 shorter events, 137.3 us)
Async XLA Ops:
  7.2 1.6 copy-start
  7.2 80.6 %all-reduce.3.cloned.1.call-start = ((), (), s32[]{:S(2)}) async-start(), calls=%async_computation | async-start | bytes 2293760 | tf_op jit(solution)/shard_map/psum | solution.py:36
  8.6 1.0 copy-start.4
  11.5 78.9 %copy-start.3 = (bf16[1,256,2240]{1,2,0:T(8,128)(2,1)S(1)}, bf16[1,256,2240]{1,2,0:T(8,128)(2,1)}, u32[]{:S(2)}) copy-start(bf16[1,256,2240]{1,2,0:T(8,128)(2,1)} %param.9) | copy-start | bytes 3440644
  11.5 200.8 %all-gather.9.cloned.1.call-start = ((), (), s32[]{:S(2)}) async-start(), calls=%async_computation.2 | async-start | bytes 34062336 | tf_op jit(solution)/shard_map/all_gather | solution.py:15
  90.3 269.9 %all-reduce.5.cloned.1.call-start = ((), (), s32[]{:S(2)}) async-start(), calls=%async_computation.1 | async-start | bytes 2064384 | tf_op jit(solution)/shard_map/psum | solution.py:43
  153.5 131.9 %copy-start.1 = (bf16[1,256,2240]{1,2,0:T(8,128)(2,1)}, bf16[1,256,2240]{1,2,0:T(8,128)(2,1)S(1)}, u32[]{:S(2)}) copy-start(bf16[1,256,2240]{1,2,0:T(8,128)(2,1)S(1)} %broadcast_maximum_fusion) | copy-start | bytes 3440644
  283.9 1.3 copy-start.9
  285.5 1.5 copy-start.6
  289.6 194.3 %all-gather.11.cloned.1.call-start = ((), (), s32[]{:S(2)}) async-start(), calls=%async_computation.3 | async-start | bytes 34062336 | tf_op jit(solution)/shard_map/all_gather | solution.py:15
  360.3 2.5 copy-start.8
  365.3 1.9 copy-start.2
  365.3 2.3 copy-start.10
  367.2 1.7 copy-start.7
  368.9 63.1 %copy-start.13 = (pred[1,256,2240]{1,2,0:T(8,128)(4,1)S(1)}, pred[1,256,2240]{1,2,0:T(8,128)(4,1)}, u32[]{:S(2)}) copy-start(pred[1,256,2240]{1,2,0:T(8,128)(4,1)} %broadcast_compare_fusion.1) | copy-start | bytes 1720324
  483.9 71.7 %copy-start.11 = (f32[112,2240]{1,0:T(8,128)S(1)}, f32[112,2240]{1,0:T(8,128)}, u32[]{:S(2)}) copy-start(f32[112,2240]{1,0:T(8,128)} %all-reduce.5.cloned.1.call-done) | copy-start | bytes 3010564
  556.6 1.7 copy-start.5
  558.3 2.4 copy-start.12
Sparse Core Ops, SparseCore 0:
  11.7 76.0 all-reduce.2
  90.9 121.4 all-gather.8
  289.7 70.4 all-reduce.4
  362.6 121.2 all-gather.10
where the time goes:
time: 576 us; the launch traced here: 570 us
  waiting for transfers between devices  253 us (44%)
  other arithmetic  153 us (27%)
  blocking collectives  123 us (21%)
  matrix products  14.4 us (2%)
  between operations  14 us (2%)
  local copies, waits for them, and re-layouts  11.9 us (2%)
    select_n x128, other arithmetic, lap(): return jax.tree.map(lambda a, b: jnp.where(reached, a, b), new, before)  143 us
    all_gather x2, waiting for transfers between devices, entering(): everything = jax.tree.map(lambda part: lax.all_gather(part, axis), array)  106 us
    all_gather x2, blocking collectives, entering(): everything = jax.tree.map(lambda part: lax.all_gather(part, axis), array)  78.2 us
    psum x1, waiting for transfers between devices, prefix_states(): totals = lax.psum((local_state, local_z), 'space')  76.1 us
    psum x1, waiting for transfers between devices, suffix_grads(): totals = lax.psum((local_grad, local_zgrad), 'space')  70.6 us
    psum x1, blocking collectives, suffix_grads(): totals = lax.psum((local_grad, local_zgrad), 'space')  23.1 us
    psum x1, blocking collectives, prefix_states(): totals = lax.psum((local_state, local_z), 'space')  22 us
  transfers between devices with their start and end apart: 4, of which 4 were waited for; matrix products, arithmetic and copies ran while one was open for 3% of the time, Pallas kernels for 0%

commit v1 on v0

v1 whole, which is shorter than its diff:
```python
import jax
import jax.numpy as jnp
from jax import lax
from jax.experimental import pallas as pl
from jax.experimental.pallas import tpu as pltpu
from jax.sharding import PartitionSpec as P

HEADS = 20
HEAD_DIM = 112
WIDTH = HEADS * HEAD_DIM
LANES = 128
ROWS = HEADS * HEAD_DIM
FRAMES = 32
SPACES = 8
TOK = 128
VMEM_LIMIT = 48 * 1024 * 1024
NN = (((1,), (0,)), ((), ()))
NT = (((1,), (1,)), ((), ()))
TN = (((0,), (0,)), ((), ()))


def mm(a, b, dims):
    return lax.dot_general(a, b, dims, preferred_element_type=jnp.float32)


def split(x):
    high = x.astype(jnp.bfloat16)
    return high, (x - high.astype(jnp.float32)).astype(jnp.bfloat16)


def head(h):
    return slice(h * HEAD_DIM, (h + 1) * HEAD_DIM)


def relu(x):
    return jnp.maximum(x, jnp.zeros_like(x))


def put_state(ref, h, value, first):
    wide = jnp.concatenate([value, jnp.zeros((HEAD_DIM, LANES - HEAD_DIM), jnp.float32)], axis=1)

    @pl.when(first)
    def _():
        ref[head(h), :] = wide

    @pl.when(jnp.logical_not(first))
    def _():
        ref[head(h), :] += wide


def state_kernel(k_ref, v_ref, state_ref, z_ref):
    first = pl.program_id(0) == 0
    total = jnp.sum(relu(k_ref[...]).astype(jnp.float32), axis=0, keepdims=True)

    @pl.when(first)
    def _():
        z_ref[...] = total

    @pl.when(jnp.logical_not(first))
    def _():
        z_ref[...] += total

    for h in range(HEADS):
        put_state(state_ref, h, mm(relu(k_ref[:, head(h)]), v_ref[:, head(h)], TN), first)


def denominators(q, z_row):
    z_wide = jnp.broadcast_to(z_row, (HEAD_DIM, HEAD_DIM))
    high, low = split(z_wide)
    return mm(q, high, NT) + mm(q, low, NT) + 1.0


def grad_kernel(q_ref, g_ref, z_ref, grad_ref):
    first = pl.program_id(0) == 0
    for h in range(HEADS):
        q = relu(q_ref[:, head(h)])
        scaled = (g_ref[:, head(h)].astype(jnp.float32) / denominators(q, z_ref[:, head(h)])).astype(jnp.bfloat16)
        put_state(grad_ref, h, mm(q, scaled, TN), first)


def query_kernel(q_ref, g_ref, z_ref, s_ref, out_ref, zgrad_ref):
    first = pl.program_id(0) == 0
    for h in range(HEADS):
        q_raw = q_ref[:, head(h)]
        q = relu(q_raw)
        z_row = z_ref[:, head(h)]
        wide = g_ref[:, head(h)].astype(jnp.float32)
        denominator = denominators(q, z_row)
        scaled = (wide / denominator).astype(jnp.bfloat16)
        high, low = split(s_ref[head(h), :HEAD_DIM])
        numerator = mm(q, high, NN) + mm(q, low, NN)
        total = jnp.sum(wide * numerator, axis=1, keepdims=True)
        denom_grad = -total / (denominator * denominator)
        direct = mm(scaled, high, NT) + mm(scaled, low, NT)
        out_ref[:, head(h)] = jnp.where(q_raw > 0, direct + denom_grad * z_row, 0.0)
        part = jnp.sum(q.astype(jnp.float32) * denom_grad, axis=0, keepdims=True)

        @pl.when(first)
        def _():
            zgrad_ref[:, head(h)] = part

        @pl.when(jnp.logical_not(first))
        def _():
            zgrad_ref[:, head(h)] += part


def key_kernel(k_ref, v_ref, sg_ref, zg_ref, key_ref, value_ref):
    for h in range(HEADS):
        k_raw = k_ref[:, head(h)]
        k = relu(k_raw)
        high, low = split(sg_ref[head(h), :HEAD_DIM])
        value_ref[:, head(h)] = mm(k, high, NN) + mm(k, low, NN)
        v = v_ref[:, head(h)]
        part = mm(v, high, NT) + mm(v, low, NT)
        key_ref[:, head(h)] = jnp.where(k_raw > 0, part + zg_ref[:, head(h)], 0.0)


TOKEN_BLOCK = pl.BlockSpec((TOK, WIDTH), lambda t: (t, 0))
STATE_BLOCK = pl.BlockSpec((ROWS, LANES), lambda t: (0, 0))
ROW_BLOCK = pl.BlockSpec((1, WIDTH), lambda t: (0, 0))
STATE_SHAPE = jax.ShapeDtypeStruct((ROWS, LANES), jnp.float32)
ROW_SHAPE = jax.ShapeDtypeStruct((1, WIDTH), jnp.float32)


def call(kernel, name, tokens, in_specs, out_specs, out_shape, flops, size):
    return pl.pallas_call(
        kernel,
        grid=(tokens // TOK,),
        in_specs=in_specs,
        out_specs=out_specs,
        out_shape=out_shape,
        name=name,
        compiler_params=pltpu.CompilerParams(vmem_limit_bytes=VMEM_LIMIT),
        cost_estimate=pl.CostEstimate(flops=flops, bytes_accessed=size, transcendentals=0),
    )


def spread(row, axis, devices):
    every = jnp.broadcast_to(row.reshape(1, 1, WIDTH), (devices, 1, WIDTH))
    return lax.all_to_all(every, axis, 0, 0, tiled=True)


def small_scan(row, reverse):
    total = jnp.sum(spread(row, "space", SPACES), axis=0)
    every = spread(total, "frame", FRAMES)
    here = lax.axis_index("frame")
    frames = lax.broadcasted_iota(jnp.int32, (FRAMES, 1, 1), 0)
    wanted = frames >= here if reverse else frames <= here
    return jnp.sum(jnp.where(wanted, every, 0.0), axis=0)


def piece_scans(state_piece, grad_piece):
    rows = state_piece.shape[0]
    padded = 9 * FRAMES
    both = jnp.stack([state_piece, grad_piece])
    both = jnp.pad(both, ((0, 0), (0, padded - rows), (0, 0)))
    slots = both.reshape(2, FRAMES, 9, LANES).transpose(1, 0, 2, 3).reshape(FRAMES, 18, LANES)
    slots = lax.all_to_all(slots, "frame", 0, 0, tiled=True)
    forward = jnp.cumsum(slots[:, :9], axis=0)
    backward = lax.cumsum(slots[:, 9:], axis=0, reverse=True)
    slots = jnp.concatenate([forward, backward], axis=1)
    slots = lax.all_to_all(slots, "frame", 0, 0, tiled=True)
    both = slots.reshape(FRAMES, 2, 9, LANES).transpose(1, 0, 2, 3).reshape(2, padded, LANES)
    return both[0, :rows], both[1, :rows]


def gather_pieces(piece):
    every = jnp.broadcast_to(piece[None], (SPACES,) + piece.shape)
    return lax.all_to_all(every, "space", 0, 0, tiled=True).reshape(ROWS, LANES)


def reduce_pieces(state):
    pieces = state.reshape(SPACES, ROWS // SPACES, LANES)
    return jnp.sum(lax.all_to_all(pieces, "space", 0, 0, tiled=True), axis=0)


def on_device(query_tokens, key_tokens, value_tokens, out_grad):
    tokens = query_tokens.shape[1]
    q, k, v, g = (a.reshape(tokens, WIDTH) for a in (query_tokens, key_tokens, value_tokens, out_grad))
    work = 2 * tokens * WIDTH * HEAD_DIM
    part = tokens * WIDTH * 2
    whole = ROWS * LANES * 4
    local_state, local_z = call(
        state_kernel, "local_state", tokens, [TOKEN_BLOCK] * 2, [STATE_BLOCK, ROW_BLOCK],
        [STATE_SHAPE, ROW_SHAPE], work, 2 * part + whole,
    )(k, v)
    state_piece = lax.psum_scatter(local_state, "space", scatter_dimension=0, tiled=True)
    zsum = small_scan(local_z, False)
    local_grad = call(
        grad_kernel, "local_grad", tokens, [TOKEN_BLOCK] * 2 + [ROW_BLOCK], STATE_BLOCK,
        STATE_SHAPE, 3 * work, 2 * part + whole,
    )(q, g, zsum)
    grad_piece = reduce_pieces(local_grad)
    state_piece, grad_piece = piece_scans(state_piece, grad_piece)
    state = gather_pieces(state_piece)
    state_grad = lax.all_gather(grad_piece, "space", axis=0, tiled=True)
    token_out = jax.ShapeDtypeStruct((tokens, WIDTH), jnp.float32)
    query_grad, local_zgrad = call(
        query_kernel, "query_grad", tokens, [TOKEN_BLOCK] * 2 + [ROW_BLOCK, STATE_BLOCK],
        [TOKEN_BLOCK, ROW_BLOCK], [token_out, ROW_SHAPE], 6 * work, 4 * part + whole,
    )(q, g, zsum, state)
    zsum_grad = small_scan(local_zgrad, True)
    key_grad, value_grad = call(
        key_kernel, "key_value_grad", tokens, [TOKEN_BLOCK] * 2 + [STATE_BLOCK, ROW_BLOCK],
        [TOKEN_BLOCK] * 2, [token_out] * 2, 4 * work, 6 * part + whole,
    )(k, v, state_grad, zsum_grad)
    return tuple(a.reshape(1, tokens, WIDTH) for a in (query_grad, key_grad, value_grad))


def solution(mesh):
    placed = P("frame", "space", None)
    return jax.shard_map(
        on_device,
        mesh=mesh,
        in_specs=(placed,) * 4,
        out_specs=(placed,) * 3,
        check_vma=False,
    )
```

time: 576 us -> 268 us (0.47)
  waiting for transfers between devices: 253 us -> 47.4 us
  other arithmetic: 153 us -> 5.72 us
  Pallas kernels: 0 us -> 65 us
  blocking collectives: 123 us -> 88.8 us
  starting transfers between devices: 0.16 us -> 19.7 us
  matrix products: 14.4 us -> 0 us
  local copies, waits for them, and re-layouts: 11.9 us -> 26.2 us
    psum x2 -> x0, waiting for transfers between devices: 147 us -> none  [the longest x1 76.1 us: prefix_states(): totals = lax.psum((local_state, local_z), 'space')]
    select_n x128 -> x0, other arithmetic: 143 us -> none  [lap(): return jax.tree.map(lambda a, b: jnp.where(reached, a, b), new, before)]
    all_gather x2 -> x1, waiting for transfers between devices: 106 us -> 0.02 us  [on_device(): state_grad = lax.all_gather(grad_piece, 'space', axis=0, tiled=True)]
    all_to_all x0 -> x5, blocking collectives: none -> 88.8 us  [the longest x1 34.4 us: reduce_pieces(): return jnp.sum(lax.all_to_all(pieces, 'space', 0, 0, tiled=True), axis=0)]
    all_gather x2 -> x0, blocking collectives: 78.2 us -> none  [entering(): everything = jax.tree.map(lambda part: lax.all_gather(part, axis), array)]
    pallas_call x0 -> x4, Pallas kernels: none -> 65 us  [the longest x1 26.7 us: on_device(): call(query_kernel, 'query_grad', tokens, [TOKEN_BLOCK] * 2 + [ROW_BLOCK,...]
    all_to_all x0 -> x3, waiting for transfers between devices: none -> 46.2 us  [the longest x1 35.4 us: gather_pieces(): return lax.all_to_all(every, 'space', 0, 0, tiled=True).reshape(ROWS, LANES)]
    psum x2 -> x0, blocking collectives: 45.2 us -> none  [the longest x1 23.1 us: suffix_grads(): totals = lax.psum((local_grad, local_zgrad), 'space')]
  transfers between devices with their start and end apart: 4 -> 5, of which waited for: 4 -> 3; matrix products, arithmetic and copies ran while one was open for 3% -> 5% of each run, Pallas kernels for 0% -> 18%
where the time goes in v1:
time: 268 us; the launch traced here: 267 us
  blocking collectives  88.8 us (33%)
  Pallas kernels  65 us (24%)
  waiting for transfers between devices  47.4 us (18%)
  local copies, waits for them, and re-layouts  26.2 us (10%)
  starting transfers between devices  19.7 us (7%)
  between operations  14.3 us (5%)
  other arithmetic  5.72 us (2%)
    all_to_all x1, waiting for transfers between devices, gather_pieces(): return lax.all_to_all(every, 'space', 0, 0, tiled=True).reshape(ROWS, LANES)  35.4 us
    all_to_all x1, blocking collectives, reduce_pieces(): return jnp.sum(lax.all_to_all(pieces, 'space', 0, 0, tiled=True), axis=0)  34.4 us
    all_to_all x2, blocking collectives, piece_scans(): slots = lax.all_to_all(slots, 'frame', 0, 0, tiled=True)  28.2 us
    pallas_call x1, Pallas kernels, on_device(): call(query_kernel, 'query_grad', tokens, [TOKEN_BLOCK] * 2 + [ROW_BLOCK,...  26.7 us
    all_to_all x2, blocking collectives, spread(): return lax.all_to_all(every, axis, 0, 0, tiled=True)  26.2 us
    unnamed x24, local copies, waits for them, and re-layouts  21.8 us
    pallas_call x1, Pallas kernels, on_device(): call(grad_kernel, 'local_grad', tokens, [TOKEN_BLOCK] * 2 + [ROW_BLOCK],...  21.1 us
    all_to_all x2, starting transfers between devices, spread(): return lax.all_to_all(every, axis, 0, 0, tiled=True)  15.2 us
  transfers between devices with their start and end apart: 5, of which 3 were waited for; matrix products, arithmetic and copies ran while one was open for 5% of the time, Pallas kernels for 18%

profile of v1, /device:TPU:1, one launch (start us, length us, event | category | flops | bytes accessed | tf_op | source)
XLA Modules:
  0.0 267.1 jit_solution(9156374214800492012)
XLA Ops:
  7.2 1.7 copy.58
  9.6 11.8 %local_state.1 = (f32[2240,128]{1,0:T(8,128)}, f32[1,2240]{1,0:T(1,128)S(1)}) custom-call(bf16[256,2240]{1,0:T(8,128)(2,1)S(1)} %bitcast.23, bf16[256,2240]{1,0:T(8,128)(2,1)S(1)} %bitcast.25), custom_call_target="tpu_custom_call" | custom-call | flops 128450560 | bytes 3440640 | tf_op jit(solution)/shard_map/local_state/pallas_call | solution.py:183
  21.5 16.2 %all_to_all.40 = f32[8,1,2240]{2,1,0:T(1,128)S(1)} all-to-all(f32[8,1,2240]{2,1,0:T(1,128)S(1)} %broadcast_in_dim.51), channel_id=1, replica_groups=mesh['frame'=32,'space'=8] {'space'}, dimensions={0} | all-to-all | bytes 143360 | tf_op jit(solution)/shard_map/all_to_all | solution.py:140
  37.8 0.9 broadcast_in_dim.52
  38.6 9.1 %all-to-all-start.1 = ((f32[32,1,2240]{2,1,0:T(1,128)}), f32[32,1,2240]{2,1,0:T(1,128)}, u32[]{:S(2)}, u32[]{:S(2)}) async-start(f32[32,1,2240]{2,1,0:T(1,128)} %broadcast_in_dim.52), calls=%async_computation.1 | async-start | bytes 589824 | tf_op jit(solution)/shard_map/all_to_all | solution.py:140
  48.5 1.6 copy.56
  50.1 2.4 copy.57
  52.5 4.6 %all-to-all-done.1 = f32[32,1,2240]{2,1,0:T(1,128)} async-done(((f32[32,1,2240]{2,1,0:T(1,128)}), f32[32,1,2240]{2,1,0:T(1,128)}, u32[]{:S(2)}, u32[]{:S(2)}) %all-to-all-start.1) | async-done | bytes 286752 | tf_op jit(solution)/shard_map/all_to_all | solution.py:140
  57.0 1.3 fusion
  58.4 1.3 copy-done
  59.7 21.1 %local_grad.1 = f32[2240,128]{1,0:T(8,128)S(1)} custom-call(bf16[256,2240]{1,0:T(8,128)(2,1)S(1)} %bitcast.27, bf16[256,2240]{1,0:T(8,128)(2,1)S(1)} %bitcast.29, f32[1,2240]{1,0:T(1,128)S(1)} %reduce_sum.51.z_ref), custom_call_target="tpu_custom_call" | custom-call | flops 385351680 | bytes 3440640 | tf_op jit(solution)/shard_map/local_grad/pallas_call | solution.py:189
  80.8 34.4 %all_to_all.41 = f32[8,280,128]{2,1,0:T(8,128)} all-to-all(f32[8,280,128]{2,1,0:T(8,128)S(1)} %bitcast.31), channel_id=1, replica_groups=mesh['frame'=32,'space'=8] {'space'}, dimensions={0} | all-to-all | bytes 2293760 | tf_op jit(solution)/shard_map/all_to_all | solution.py:174
  115.2 2.0 reduce_sum.52
  117.2 1.0 pad_maximum_fusion.1
  118.7 14.5 %all_to_all.42 = f32[32,18,128]{2,1,0:T(8,128)S(1)} all-to-all(f32[32,18,128]{2,1,0:T(8,128)S(1)} %copy.64), channel_id=1, replica_groups=mesh['frame'=32,'space'=8] {'frame'}, dimensions={0} | all-to-all | bytes 589824 | tf_op jit(solution)/shard_map/all_to_all | solution.py:158
  133.5 13.7 %all_to_all.43 = f32[32,18,128]{2,1,0:T(8,128)S(1)} all-to-all(f32[32,18,128]{2,1,0:T(8,128)S(1)} %pad_maximum_fusion), channel_id=1, replica_groups=mesh['frame'=32,'space'=8] {'frame'}, dimensions={0} | all-to-all | bytes 589824 | tf_op jit(solution)/shard_map/all_to_all | solution.py:162
  147.4 0.9 fusion.6
  148.3 1.1 broadcast_in_dim.55
  149.4 4.2 %all-to-all-start.5 = ((f32[8,280,128]{2,1,0:T(8,128)}), f32[8,280,128]{2,1,0:T(8,128)}, u32[]{:S(2)}, u32[]{:S(2)}) async-start(f32[8,280,128]{2,1,0:T(8,128)} %broadcast_in_dim.55), calls=%async_computation.5 | async-start | bytes 2293760 | tf_op jit(solution)/shard_map/all_to_all | solution.py:169
  154.4 35.4 %all-to-all-done.5 = f32[8,280,128]{2,1,0:T(8,128)} async-done(((f32[8,280,128]{2,1,0:T(8,128)}), f32[8,280,128]{2,1,0:T(8,128)}, u32[]{:S(2)}, u32[]{:S(2)}) %all-to-all-start.5) | async-done | bytes 1146912 | tf_op jit(solution)/shard_map/all_to_all | solution.py:169
  189.8 1.3 copy-done.1
  191.0 26.7 %query_grad.1 = (f32[256,2240]{1,0:T(8,128)S(1)}, f32[1,2240]{1,0:T(1,128)S(1)}) custom-call(bf16[256,2240]{1,0:T(8,128)(2,1)S(1)} %bitcast.28, bf16[256,2240]{1,0:T(8,128)(2,1)S(1)} %bitcast.30, f32[1,2240]{1,0:T(1,128)S(1)} %reduce_sum.51.z_ref, f32[2240,128]{1,0:T(8,128)} %bitcast.15.s_ref), custom_call_target="tpu_custom_call" | custom-call | flops 770703360 | bytes 5734400 | tf_op jit(solution)/shard_map/query_grad/pallas_call | solution.py:198
  217.8 1.4 copy-done.2
  220.6 10.0 %all_to_all.44 = f32[8,1,2240]{2,1,0:T(1,128)S(1)} all-to-all(f32[8,1,2240]{2,1,0:T(1,128)S(1)} %broadcast_in_dim.58), channel_id=1, replica_groups=mesh['frame'=32,'space'=8] {'space'}, dimensions={0} | all-to-all | bytes 143360 | tf_op jit(solution)/shard_map/all_to_all | solution.py:140
  231.5 6.1 %all-to-all-start.7 = ((f32[32,1,2240]{2,1,0:T(1,128)}), f32[32,1,2240]{2,1,0:T(1,128)S(1)}, u32[]{:S(2)}, u32[]{:S(2)}) async-start(f32[32,1,2240]{2,1,0:T(1,128)} %broadcast_in_dim.59), calls=%async_computation.7 | async-start | bytes 589824 | tf_op jit(solution)/shard_map/all_to_all | solution.py:140
  237.6 3.0 %copy.70 = f32[1,256,2240]{1,2,0:T(8,128)} copy(f32[1,256,2240]{2,1,0:T(8,128)} %bitcast.32) | data formatting | bytes 4587520
  240.6 6.3 %all-to-all-done.7 = f32[32,1,2240]{2,1,0:T(1,128)S(1)} async-done(((f32[32,1,2240]{2,1,0:T(1,128)}), f32[32,1,2240]{2,1,0:T(1,128)S(1)}, u32[]{:S(2)}, u32[]{:S(2)}) %all-to-all-start.7) | async-done | bytes 286752 | tf_op jit(solution)/shard_map/all_to_all | solution.py:140
  247.3 1.2 copy-done.4
  248.5 5.3 %key_value_grad.1 = (f32[256,2240]{1,0:T(8,128)S(1)}, f32[256,2240]{1,0:T(8,128)}) custom-call(bf16[256,2240]{1,0:T(8,128)(2,1)S(1)} %bitcast.24, bf16[256,2240]{1,0:T(8,128)(2,1)S(1)} %bitcast.26, f32[2240,128]{1,0:T(8,128)S(1)} %bitcast.34, f32[1,2240]{1,0:T(1,128)S(1)} %reduce_sum.55.zg_ref), custom_call_target="tpu_custom_call" | custom-call | flops 513802240 | bytes 8028160 | tf_op jit(solution)/shard_map/key_value_grad/pallas_call | solution.py:203
  253.8 1.4 copy-done.3
  255.2 3.2 %copy.71 = f32[1,256,2240]{1,2,0:T(8,128)} copy(f32[1,256,2240]{2,1,0:T(8,128)} %bitcast.33) | data formatting | bytes 4587520
  258.4 1.9 copy.72
  (39 shorter events, 6.0 us)
Async XLA Ops:
  7.2 1.7 copy-start.7
  38.6 18.4 %all-to-all-start.1 = ((f32[32,1,2240]{2,1,0:T(1,128)}), f32[32,1,2240]{2,1,0:T(1,128)}, u32[]{:S(2)}, u32[]{:S(2)}) async-start(f32[32,1,2240]{2,1,0:T(1,128)} %broadcast_in_dim.52), calls=%async_computation.1 | async-start | bytes 589824 | tf_op jit(solution)/shard_map/all_to_all | solution.py:140
  47.8 69.5 %reduce-scatter.4.cloned.1.call-start = ((), (), s32[]{:S(2)}) async-start(), calls=%async_computation.10 | async-start | bytes 1290240
  58.3 1.3 copy-start
  149.4 40.4 %all-to-all-start.5 = ((f32[8,280,128]{2,1,0:T(8,128)}), f32[8,280,128]{2,1,0:T(8,128)}, u32[]{:S(2)}, u32[]{:S(2)}) async-start(f32[8,280,128]{2,1,0:T(8,128)} %broadcast_in_dim.55), calls=%async_computation.5 | async-start | bytes 2293760 | tf_op jit(solution)/shard_map/all_to_all | solution.py:169
  153.6 93.6 %all-gather.3.cloned.1.call-start = ((), (), s32[]{:S(2)}) async-start(), calls=%async_computation.9 | async-start | bytes 1290240 | tf_op jit(solution)/shard_map/all_gather | solution.py:196
  189.8 1.3 copy-start.1
  217.8 1.4 copy-start.2
  219.2 0.6 copy-start.5
  231.5 15.4 %all-to-all-start.7 = ((f32[32,1,2240]{2,1,0:T(1,128)}), f32[32,1,2240]{2,1,0:T(1,128)S(1)}, u32[]{:S(2)}, u32[]{:S(2)}) async-start(f32[32,1,2240]{2,1,0:T(1,128)} %broadcast_in_dim.59), calls=%async_computation.7 | async-start | bytes 589824 | tf_op jit(solution)/shard_map/all_to_all | solution.py:140
  247.3 1.3 copy-start.4
  253.8 1.4 copy-start.3
  255.2 3.2 %copy-start.6 = (f32[256,2240]{1,0:T(8,128)S(1)}, f32[256,2240]{1,0:T(8,128)}, u32[]{:S(2)}) copy-start(f32[256,2240]{1,0:T(8,128)} %get-tuple-element.14) | copy-start | bytes 6881284
Sparse Core Ops, SparseCore 0:
  51.7 31.3 reduce-scatter.3
  156.2 41.3 all-gather.2
